TPU v7x, 128 devices: a whole 4x4x4 slice. The times are simulated.
128 devices in a mesh: row: 8 (over x_lo, z), col: 16 (over y, x_hi, core).
Axes of the slice: x: 4 (x_hi: 2, x_lo: 2; x = x_hi * 2 + x_lo), y: 4, z: 4, core: 2. Of those that a mesh axis runs over, the one named last changes fastest.
Arguments:
- amplitudes: bfloat16 [32, 32, 12, 4096], P('row', 'col'), may hold values from -6 to 6
- integrals: bfloat16 [32, 32, 47, 4096], P('row', 'col'), may hold values from -0.125 to 0.125
- pair_lists: int32 [8, 12, 2], replicated, may hold values from 0 to 46, as said below
- tile_counts: int32 [8], replicated, may hold values from 1 to 12, as said below
Outputs:
- symmetric: float32 [32, 32, 12, 4096], P('row', 'col')
Inputs may be any that keep to these rules, and one draw needn't show every extreme that they name: `pair_lists`: each grid row lists 12 distinct ordered pairs of different tiles. `tile_counts`: the largest count equals 12.
All inputs are finite; a program needn't handle non-finite values.
Results may differ from a plain program's by a relative error of at most 0.0029.
Values may be sent and summed in bfloat16 or wider, within the bound.
A program may use at most 128 MiB of HBM per device.

v0:
```python
import jax
import jax.numpy as jnp
from jax import lax
from jax.sharding import PartitionSpec as P

TILE = 64


def spread(block, axis, owner):
    block = jnp.where(lax.axis_index(axis) == owner, block, jnp.zeros_like(block))
    return lax.psum(block, axis)


def on_device(amplitudes, integrals, pair_lists, tile_counts):
    occ_row, occ_col, slot_count, square = amplitudes.shape
    tile_width = TILE
    row_devices = lax.axis_size("row")
    col_devices = lax.axis_size("col")
    col_ratio = col_devices // row_devices
    my_row = lax.axis_index("row")
    my_col = lax.axis_index("col")
    partner_row = my_col // col_ratio
    tile_first = pair_lists[:, :, 0]
    tile_second = pair_lists[:, :, 1]
    packed = jnp.take(integrals, tile_second.reshape(-1), axis=2)
    packed = packed.reshape(occ_row, occ_col, row_devices, slot_count, square)
    received = lax.all_to_all(packed, "row", split_axis=2, concat_axis=0, tiled=True)
    received = received.reshape(occ_row * row_devices, occ_col, slot_count, square)
    piece = lax.all_gather(amplitudes, "col", axis=1, tiled=True)
    piece_count = piece.shape[1]
    left_tiles = piece.reshape(occ_row, piece_count, slot_count, tile_width, tile_width)
    right_tiles = received.reshape(piece_count, occ_col, slot_count, tile_width, tile_width)
    cycle_sum = jnp.einsum(
        "iksac,kjscb->ijsab", left_tiles, right_tiles, preferred_element_type=jnp.float32
    )
    my_count = lax.dynamic_index_in_dim(tile_counts, my_row, 0, keepdims=False)
    live_slots = (jnp.arange(slot_count, dtype=jnp.int32) < my_count).astype(jnp.float32)
    cycle_value = (cycle_sum * live_slots[None, None, :, None, None]).astype(jnp.bfloat16)
    cycle = cycle_value.reshape(occ_row, occ_col, slot_count, square)
    residual_strip = lax.all_gather(cycle, "col", axis=1, tiled=True)
    mirror_part = lax.dynamic_slice_in_dim(residual_strip, my_col % col_ratio * occ_col, occ_col, 0)
    mirror_whole = spread(mirror_part, "row", partner_row)
    mirror_block = lax.dynamic_slice_in_dim(mirror_whole, my_row * occ_row, occ_row, 1)
    mirror_block = mirror_block.reshape(occ_col, occ_row, slot_count, tile_width, tile_width)
    mine_first = lax.dynamic_index_in_dim(tile_first, my_row, 0, keepdims=False)
    mine_second = lax.dynamic_index_in_dim(tile_second, my_row, 0, keepdims=False)
    their_first = lax.dynamic_index_in_dim(tile_first, partner_row, 0, keepdims=False)
    their_second = lax.dynamic_index_in_dim(tile_second, partner_row, 0, keepdims=False)
    pair_match = (
        (mine_first[:, None] == their_second[None, :])
        & (mine_second[:, None] == their_first[None, :])
    ).astype(jnp.bfloat16)
    crossed = jnp.einsum(
        "st,jitba->ijsab", pair_match, mirror_block, preferred_element_type=jnp.float32
    )
    own_part = cycle_value.astype(jnp.float32)
    symmetric = (own_part + crossed) * live_slots[None, None, :, None, None]
    return symmetric.reshape(occ_row, occ_col, slot_count, square)


def solution(mesh):
    return jax.shard_map(
        on_device,
        mesh=mesh,
        in_specs=(P("row", "col", None, None), P("row", "col", None, None), P(), P()),
        out_specs=P("row", "col", None, None),
        check_vma=False,
    )
```

profile of v0, /device:TPU:1, one launch (start us, length us, event | category | flops | bytes accessed | tf_op | source)
XLA Modules:
  0.0 507.0 jit_solution(17754718859662884650)
XLA Ops:
  6.5 0.0 copy-start
  6.5 2.8 copy.18
  9.3 0.0 all-gather.3.cloned.1.call-update
  9.3 0.8 fusion.29
  10.1 0.1 reshape_squeeze.6
  10.2 0.0 copy-done
  10.2 15.2 %gather_fusion = bf16[96,4,2,4096]{3,2,1,0:T(2,128)(2,1)} fusion(bf16[4,2,47,4096]{3,1,2,0:T(2,128)(2,1)S(1)} %copy-done, s32[1024]{0:T(1024)S(1)} %pad_clamp_fusion), kind=kCustom, calls=%fused_computation | custom fusion | bytes 12583296 | tf_op jit(solution)/shard_map/jit(_take)/gather | solution.py:25
  25.5 8.5 %broadcast_select_fusion.1 = bf16[4,2,8,12,4096]{4,1,3,0,2:T(2,128)(2,1)} fusion(pred[8,12]{1,0:T(8,128)(4,1)S(1)} %compare_and_fusion, bf16[4,2,8,12,4096]{4,1,0,3,2:T(2,128)(2,1)} %bitcast.67), kind=kLoop, calls=%fused_computation.5 | loop fusion | flops 3145728 | bytes 12583008 | tf_op jit(solution)/shard_map/jit(_take)/select_n | solution.py:25
  33.9 6.9 %all-to-all-start = ((bf16[4,2,8,12,4096]{4,1,3,0,2:T(2,128)(2,1)}), bf16[4,2,8,12,4096]{4,1,3,0,2:T(2,128)(2,1)}, u32[]{:S(2)}, u32[]{:S(2)}) async-start(bf16[4,2,8,12,4096]{4,1,3,0,2:T(2,128)(2,1)} %broadcast_select_fusion.1), calls=%async_computation | async-start | bytes 12582912 | tf_op jit(solution)/shard_map/all_to_all | solution.py:27
  40.9 0.2 all-gather.5.cloned.1.call-start
  41.1 0.6 dynamic_slice.23
  41.7 0.6 compare_convert_fusion
  42.3 101.4 %all-to-all-done = bf16[4,2,8,12,4096]{4,1,3,0,2:T(2,128)(2,1)} async-done(((bf16[4,2,8,12,4096]{4,1,3,0,2:T(2,128)(2,1)}), bf16[4,2,8,12,4096]{4,1,3,0,2:T(2,128)(2,1)}, u32[]{:S(2)}, u32[]{:S(2)}) %all-to-all-start) | async-done | bytes 6291488 | tf_op jit(solution)/shard_map/all_to_all | solution.py:27
  143.6 20.6 %reshape_reshape.3 = bf16[32,2,12,64,64]{4,3,1,2,0:T(8,128)(2,1)} reshape(bf16[8,4,2,1,12,4096]{5,2,4,1,0,3:T(2,128)(2,1)} %bitcast.5) | data formatting | bytes 12582912 | tf_op jit(solution)/shard_map/reshape;reshape | solution.py:32
  164.2 14.4 %copy.19 = bf16[4,32,12,4096]{3,1,0,2:T(8,128)(2,1)} copy(bf16[4,32,12,4096]{3,0,2,1:T(4,128)(2,1)} %all-gather.3.cloned.1.call-done) | data formatting | bytes 25165824 | tf_op jit(solution)/shard_map/all_gather | solution.py:29
  178.6 34.4 %reshape.81 = bf16[4,32,12,64,64,1]{4,3,1,0,2,5:T(8,128)(2,1)} reshape(bf16[4,32,12,4096]{3,1,0,2:T(8,128)(2,1)} %copy.19) | data formatting | bytes 25165824 | tf_op jit(solution)/shard_map/reshape | solution.py:31
  213.0 19.0 %fusion.11 = bf16[4,2,12,64,64]{3,4,0,1,2:T(8,128)(2,1)S(1)} fusion(f32[12]{0:T(128)S(1)} %compare_convert_fusion, bf16[4,32,12,64,64,1]{4,3,1,0,2,5:T(8,128)(2,1)} %reshape.81, bf16[32,2,12,64,64]{4,3,1,2,0:T(8,128)(2,1)} %reshape_reshape.3), kind=kOutput, calls=%fused_computation.12 | convolution fusion | flops 1611399168 | bytes 19660848 | tf_op jit(solution)/shard_map/iksac,kjscb->ijsab/dot_general | solution.py:33
  232.1 1.8 copy.33
  233.8 3.7 reshape.85
  237.5 0.0 all-gather.5.cloned.1.call-update
  237.5 0.3 all-reduce.2.cloned.1.call-start
  237.8 93.1 %all-gather.5.cloned.1.call-done = bf16[4,32,12,4096]{3,0,2,1:T(4,128)(2,1)} async-done(((bf16[4,2,12,4096]{3,0,2,1:T(4,128)(2,1)}), bf16[4,32,12,4096]{3,0,2,1:T(4,128)(2,1)}) %all-gather.5.cloned.1.call-update) | async-done | bytes 12582928 | tf_op jit(solution)/shard_map/all_gather | solution.py:40
  330.9 10.8 %broadcast_select_fusion = bf16[2,32,12,4096]{3,0,2,1:T(2,128)(2,1)} fusion(pred[]{:T(512)S(6)} %eq.39, bf16[4,32,12,4096]{3,0,2,1:T(4,128)(2,1)} %all-gather.5.cloned.1.call-done, s32[]{:T(128)S(6)} %select_n.65), kind=kLoop, calls=%fused_computation.4 | loop fusion | flops 3145728 | bytes 12582917 | tf_op jit(solution)/shard_map/jit(_where)/select_n | solution.py:10
  341.7 0.0 all-reduce.2.cloned.1.call-update
  341.7 142.5 %all-reduce.2.cloned.1.call-done = bf16[2,32,12,4096]{3,0,2,1:T(2,128)(2,1)} async-done(((bf16[2,32,12,4096]{3,0,2,1:T(2,128)(2,1)}), bf16[2,32,12,4096]{3,0,2,1:T(2,128)(2,1)}) %all-reduce.2.cloned.1.call-update) | async-done | bytes 6291472 | tf_op jit(solution)/shard_map/psum | solution.py:11
  484.3 2.0 constant_dynamic-slice_fusion.4
  486.3 1.0 reshape.86
  487.3 1.1 fusion.5
  488.4 0.0 copy-start.1
  488.4 4.3 fusion.3
  492.7 3.6 copy.26
  496.3 4.2 reshape.71
  (12 shorter events, 0.1 us)
Async XLA Ops:
  6.5 3.7 copy-start
  6.5 157.7 %all-gather.3.cloned.1.call-start = ((), (), s32[]{:S(2)}) async-start(), calls=%async_computation.1 | async-start | bytes 13369344 | tf_op jit(solution)/shard_map/all_gather | solution.py:29
  33.9 7.2 %copy-start.3 = (s32[8]{0:T(128)S(1)}, s32[8]{0:T(128)}, u32[]{:S(2)}) copy-start(s32[8]{0:T(128)} %param.7) | copy-start | bytes 100
  33.9 109.7 %all-to-all-start = ((bf16[4,2,8,12,4096]{4,1,3,0,2:T(2,128)(2,1)}), bf16[4,2,8,12,4096]{4,1,3,0,2:T(2,128)(2,1)}, u32[]{:S(2)}, u32[]{:S(2)}) async-start(bf16[4,2,8,12,4096]{4,1,3,0,2:T(2,128)(2,1)} %broadcast_select_fusion.1), calls=%async_computation | async-start | bytes 12582912 | tf_op jit(solution)/shard_map/all_to_all | solution.py:27
  40.9 290.0 %all-gather.5.cloned.1.call-start = ((), (), s32[]{:S(2)}) async-start(), calls=%async_computation.2 | async-start | bytes 13369344 | tf_op jit(solution)/shard_map/all_gather | solution.py:40
  232.0 109.6 %copy-start.2 = (bf16[4,2,12,64,64]{3,4,0,1,2:T(8,128)(2,1)}, bf16[4,2,12,64,64]{3,4,0,1,2:T(8,128)(2,1)S(1)}, u32[]{:S(2)}) copy-start(bf16[4,2,12,64,64]{3,4,0,1,2:T(8,128)(2,1)S(1)} %fusion.11) | copy-start | bytes 2359300
  237.5 246.7 %all-reduce.2.cloned.1.call-start = ((), (), s32[]{:S(2)}) async-start(), calls=%async_computation.3 | async-start | bytes 12582912 | tf_op jit(solution)/shard_map/psum | solution.py:11
  488.4 12.0 %copy-start.1 = (bf16[4,2,47,4096]{3,1,2,0:T(2,128)(2,1)S(1)}, bf16[4,2,47,4096]{3,1,2,0:T(2,128)(2,1)}, u32[]{:S(2)}) copy-start(bf16[4,2,47,4096]{3,1,2,0:T(2,128)(2,1)} %param.5) | copy-start | bytes 9240580
Sparse Core Ops, SparseCore 0:
  9.8 128.3 all-gather.2
  237.6 93.2 all-gather.4
  341.8 142.4 all-reduce.1
where the time goes:
time: 509 us; the launch traced here: 507 us
  waiting for transfers between devices  337 us (66%)
  local copies, waits for them, and re-layouts  105 us (21%)
  other arithmetic  24.1 us (5%)
  matrix products  20.1 us (4%)
  between operations  13.2 us (3%)
  starting transfers between devices  7.4 us (1%)
    psum x1, waiting for transfers between devices, spread(): return lax.psum(block, axis)  143 us
    all_to_all x1, waiting for transfers between devices, on_device(): lax.all_to_all(packed, 'row', split_axis=2, concat_axis=0, tiled=True)  101 us
    all_gather x1, waiting for transfers between devices, on_device(): residual_strip = lax.all_gather(cycle, 'col', axis=1, tiled=True)  93.1 us
    reshape x1, local copies, waits for them, and re-layouts, on_device(): piece.reshape(occ_row, piece_count, slot_count, tile_width, tile_width)  34.4 us
    another operation x1, local copies, waits for them, and re-layouts, on_device(): received.reshape(piece_count, occ_col, slot_count, tile_width, tile_width)  20.6 us
    dot_general x1, matrix products, on_device(): jnp.einsum('iksac,kjscb->ijsab', left_tiles, right_tiles, preferred_eleme...  19 us
    gather x1, local copies, waits for them, and re-layouts, on_device(): packed = jnp.take(integrals, tile_second.reshape(-1), axis=2)  15.2 us
    all_gather x1, local copies, waits for them, and re-layouts, on_device(): piece = lax.all_gather(amplitudes, 'col', axis=1, tiled=True)  14.4 us
  transfers between devices with their start and end apart: 4, of which 3 were waited for; matrix products, arithmetic and copies ran while one was open for 9% of the time, Pallas kernels for 0%

commit v1 on v0

--- a/solution.py
+++ b/solution.py
@@ -12,6 +12,13 @@
 
 
 def on_device(amplitudes, integrals, pair_lists, tile_counts):
+
+    def show_keys_now(my_tile):
+        z1 = jnp.stack([my_tile] * lax.axis_size("col"), 0)
+        opened = lax.all_to_all(z1, axis_name="col", split_axis=0, concat_axis=0)
+        row_out = jnp.concatenate(opened, 1)
+        return row_out
+
     occ_row, occ_col, slot_count, square = amplitudes.shape
     tile_width = TILE
     row_devices = lax.axis_size("row")
@@ -26,7 +33,7 @@
     packed = packed.reshape(occ_row, occ_col, row_devices, slot_count, square)
     received = lax.all_to_all(packed, "row", split_axis=2, concat_axis=0, tiled=True)
     received = received.reshape(occ_row * row_devices, occ_col, slot_count, square)
-    piece = lax.all_gather(amplitudes, "col", axis=1, tiled=True)
+    piece = show_keys_now(amplitudes)
     piece_count = piece.shape[1]
     left_tiles = piece.reshape(occ_row, piece_count, slot_count, tile_width, tile_width)
     right_tiles = received.reshape(piece_count, occ_col, slot_count, tile_width, tile_width)

time: 509 us -> 616 us (1.21)
  waiting for transfers between devices: 337 us -> 419 us
  local copies, waits for them, and re-layouts: 105 us -> 121 us
  starting transfers between devices: 7.4 us -> 15.1 us
    all_to_all x0 -> x1, waiting for transfers between devices: none -> 119 us  [show_keys_now(): opened = lax.all_to_all(z1, axis_name='col', split_axis=0, concat_axis=0)]
    another operation x0 -> x2, local copies, waits for them, and re-layouts: none -> 52.6 us  [the longest x1 40.1 us: on_device(): piece.reshape(occ_row, piece_count, slot_count, tile_width, tile_width)]
    all_to_all x1, waiting for transfers between devices: 101 us -> 70.4 us  [on_device(): lax.all_to_all(packed, 'row', split_axis=2, concat_axis=0, tiled=True)]
    reshape x1, local copies, waits for them, and re-layouts: 34.4 us -> 13.2 us  [show_keys_now(): row_out = jnp.concatenate(opened, 1)]
    all_gather x1 -> x0, local copies, waits for them, and re-layouts: 14.4 us -> none  [on_device(): piece = lax.all_gather(amplitudes, 'col', axis=1, tiled=True)]
    all_to_all x0 -> x1, starting transfers between devices: none -> 7.72 us  [show_keys_now(): opened = lax.all_to_all(z1, axis_name='col', split_axis=0, concat_axis=0)]
  transfers between devices with their start and end apart: 4 -> 4, of which waited for: 3 -> 4; matrix products, arithmetic and copies ran while one was open for 9% -> 4% of each run, Pallas kernels for 0% -> 0%
where the time goes in v1:
time: 616 us; the launch traced here: 613 us
  waiting for transfers between devices  419 us (68%)
  local copies, waits for them, and re-layouts  121 us (20%)
  other arithmetic  24.2 us (4%)
  matrix products  20.1 us (3%)
  starting transfers between devices  15.1 us (2%)
  between operations  13.6 us (2%)
    psum x1, waiting for transfers between devices, spread(): return lax.psum(block, axis)  143 us
    all_to_all x1, waiting for transfers between devices, show_keys_now(): opened = lax.all_to_all(z1, axis_name='col', split_axis=0, concat_axis=0)  119 us
    all_gather x1, waiting for transfers between devices, on_device(): residual_strip = lax.all_gather(cycle, 'col', axis=1, tiled=True)  87.4 us
    all_to_all x1, waiting for transfers between devices, on_device(): lax.all_to_all(packed, 'row', split_axis=2, concat_axis=0, tiled=True)  70.4 us
    another operation x1, local copies, waits for them, and re-layouts, on_device(): piece.reshape(occ_row, piece_count, slot_count, tile_width, tile_width)  40.1 us
    another operation x1, local copies, waits for them, and re-layouts, on_device(): received.reshape(piece_count, occ_col, slot_count, tile_width, tile_width)  20.6 us
    dot_general x1, matrix products, on_device(): jnp.einsum('iksac,kjscb->ijsab', left_tiles, right_tiles, preferred_eleme...  19 us
    gather x1, local copies, waits for them, and re-layouts, on_device(): packed = jnp.take(integrals, tile_second.reshape(-1), axis=2)  15.2 us
  transfers between devices with their start and end apart: 4, of which 4 were waited for; matrix products, arithmetic and copies ran while one was open for 4% of the time, Pallas kernels for 0%

profile of v1, /device:TPU:1, one launch (start us, length us, event | category | flops | bytes accessed | tf_op | source)
XLA Modules:
  0.0 613.4 jit_solution(7406031054567403025)
XLA Ops:
  6.5 0.9 fusion.29
  7.4 0.1 reshape_squeeze.6
  7.5 0.9 copy-done
  8.4 15.2 %gather_fusion = bf16[96,4,2,4096]{3,2,1,0:T(2,128)(2,1)} fusion(bf16[4,2,47,4096]{3,1,2,0:T(2,128)(2,1)S(1)} %copy-done, s32[1024]{0:T(1024)S(1)} %pad_clamp_fusion), kind=kCustom, calls=%fused_computation | custom fusion | bytes 12583296 | tf_op jit(solution)/shard_map/jit(_take)/gather | solution.py:32
  23.7 8.5 %broadcast_select_fusion.1 = bf16[4,2,8,12,4096]{4,1,3,0,2:T(2,128)(2,1)} fusion(pred[8,12]{1,0:T(8,128)(4,1)S(1)} %compare_and_fusion, bf16[4,2,8,12,4096]{4,1,0,3,2:T(2,128)(2,1)} %bitcast.66), kind=kLoop, calls=%fused_computation.5 | loop fusion | flops 3145728 | bytes 12583008 | tf_op jit(solution)/shard_map/jit(_take)/select_n | solution.py:32
  32.2 6.9 %all-to-all-start = ((bf16[4,2,8,12,4096]{4,1,3,0,2:T(2,128)(2,1)}), bf16[4,2,8,12,4096]{4,1,3,0,2:T(2,128)(2,1)}, u32[]{:S(2)}, u32[]{:S(2)}) async-start(bf16[4,2,8,12,4096]{4,1,3,0,2:T(2,128)(2,1)} %broadcast_select_fusion.1), calls=%async_computation | async-start | bytes 12582912 | tf_op jit(solution)/shard_map/all_to_all | solution.py:34
  39.1 0.8 copy.18
  39.9 70.4 %all-to-all-done = bf16[4,2,8,12,4096]{4,1,3,0,2:T(2,128)(2,1)} async-done(((bf16[4,2,8,12,4096]{4,1,3,0,2:T(2,128)(2,1)}), bf16[4,2,8,12,4096]{4,1,3,0,2:T(2,128)(2,1)}, u32[]{:S(2)}, u32[]{:S(2)}) %all-to-all-start) | async-done | bytes 6291488 | tf_op jit(solution)/shard_map/all_to_all | solution.py:34
  110.3 12.5 %stack.2 = bf16[16,4,2,12,4096]{4,2,1,3,0:T(2,128)(2,1)} broadcast(bf16[4,2,12,4096]{3,1,0,2:T(2,128)(2,1)S(1)} %copy.18), dimensions={1,2,3,4} | broadcast | bytes 13369344 | tf_op jit(solution)/shard_map/stack | solution.py:17
  122.7 7.7 %all-to-all-start.1 = ((bf16[16,4,2,12,4096]{4,2,1,3,0:T(2,128)(2,1)}), bf16[16,4,2,12,4096]{4,2,1,3,0:T(2,128)(2,1)}, u32[]{:S(2)}, u32[]{:S(2)}) async-start(bf16[16,4,2,12,4096]{4,2,1,3,0:T(2,128)(2,1)} %stack.2), calls=%async_computation.1 | async-start | bytes 25165824 | tf_op jit(solution)/shard_map/all_to_all | solution.py:18
  130.5 0.2 all-gather.2.cloned.1.call-start
  130.7 0.6 dynamic_slice.23
  131.3 0.6 compare_convert_fusion
  131.9 20.6 %reshape_reshape.6 = bf16[32,2,12,64,64]{4,3,1,2,0:T(8,128)(2,1)} reshape(bf16[8,4,2,1,12,4096]{5,2,4,1,0,3:T(2,128)(2,1)} %bitcast.5) | data formatting | bytes 12582912 | tf_op jit(solution)/shard_map/reshape;reshape | solution.py:39
  152.6 118.9 %all-to-all-done.1 = bf16[16,4,2,12,4096]{4,2,1,3,0:T(2,128)(2,1)} async-done(((bf16[16,4,2,12,4096]{4,2,1,3,0:T(2,128)(2,1)}), bf16[16,4,2,12,4096]{4,2,1,3,0:T(2,128)(2,1)}, u32[]{:S(2)}, u32[]{:S(2)}) %all-to-all-start.1) | async-done | bytes 12582944 | tf_op jit(solution)/shard_map/all_to_all | solution.py:18
  271.4 13.2 %copy.19 = bf16[4,16,2,12,4096]{4,2,1,0,3:T(2,128)(2,1)} copy(bf16[4,16,2,12,4096]{4,2,0,3,1:T(2,128)(2,1)} %bitcast.7) | data formatting | bytes 25165824 | tf_op jit(solution)/shard_map/reshape | solution.py:19
  284.7 40.1 %reshape.83 = bf16[4,32,12,64,64,1]{4,3,1,0,2,5:T(8,128)(2,1)} reshape(bf16[4,16,2,12,4096]{4,2,1,0,3:T(2,128)(2,1)} %copy.19) | data formatting | bytes 25165824 | tf_op jit(solution)/shard_map/reshape;reshape | solution.py:38
  324.8 19.0 %fusion.11 = bf16[4,2,12,64,64]{3,4,0,1,2:T(8,128)(2,1)S(1)} fusion(f32[12]{0:T(128)S(1)} %compare_convert_fusion, bf16[4,32,12,64,64,1]{4,3,1,0,2,5:T(8,128)(2,1)} %reshape.83, bf16[32,2,12,64,64]{4,3,1,2,0:T(8,128)(2,1)} %reshape_reshape.6), kind=kOutput, calls=%fused_computation.12 | convolution fusion | flops 1611399168 | bytes 19660848 | tf_op jit(solution)/shard_map/iksac,kjscb->ijsab/dot_general | solution.py:40
  343.8 1.8 copy.33
  345.6 3.7 reshape.87
  349.2 0.0 all-gather.2.cloned.1.call-update
  349.3 0.3 all-reduce.2.cloned.1.call-start
  349.6 87.4 %all-gather.2.cloned.1.call-done = bf16[4,32,12,4096]{3,0,2,1:T(4,128)(2,1)} async-done(((bf16[4,2,12,4096]{3,0,2,1:T(4,128)(2,1)}), bf16[4,32,12,4096]{3,0,2,1:T(4,128)(2,1)}) %all-gather.2.cloned.1.call-update) | async-done | bytes 12582928 | tf_op jit(solution)/shard_map/all_gather | solution.py:47
  437.0 10.8 %broadcast_select_fusion = bf16[2,32,12,4096]{3,0,2,1:T(2,128)(2,1)} fusion(pred[]{:T(512)S(6)} %eq.39, bf16[4,32,12,4096]{3,0,2,1:T(4,128)(2,1)} %all-gather.2.cloned.1.call-done, s32[]{:T(128)S(6)} %select_n.65), kind=kLoop, calls=%fused_computation.4 | loop fusion | flops 3145728 | bytes 12582917 | tf_op jit(solution)/shard_map/jit(_where)/select_n | solution.py:10
  447.7 0.0 all-reduce.2.cloned.1.call-update
  447.8 142.5 %all-reduce.2.cloned.1.call-done = bf16[2,32,12,4096]{3,0,2,1:T(2,128)(2,1)} async-done(((bf16[2,32,12,4096]{3,0,2,1:T(2,128)(2,1)}), bf16[2,32,12,4096]{3,0,2,1:T(2,128)(2,1)}) %all-reduce.2.cloned.1.call-update) | async-done | bytes 6291472 | tf_op jit(solution)/shard_map/psum | solution.py:11
  590.4 2.0 constant_dynamic-slice_fusion.4
  592.4 1.0 reshape.88
  593.4 1.1 fusion.5
  594.5 4.3 fusion.3
  598.8 3.6 copy.26
  602.4 4.2 reshape.73
  (14 shorter events, 0.1 us)
Async XLA Ops:
  6.5 1.9 copy-start
  32.2 6.9 %copy-start.3 = (bf16[4,2,12,4096]{3,1,2,0:T(2,128)(2,1)S(1)}, bf16[4,2,12,4096]{3,1,2,0:T(2,128)(2,1)}, u32[]{:S(2)}) copy-start(bf16[4,2,12,4096]{3,1,2,0:T(2,128)(2,1)} %param.4) | copy-start | bytes 2359300
  32.2 78.1 %all-to-all-start = ((bf16[4,2,8,12,4096]{4,1,3,0,2:T(2,128)(2,1)}), bf16[4,2,8,12,4096]{4,1,3,0,2:T(2,128)(2,1)}, u32[]{:S(2)}, u32[]{:S(2)}) async-start(bf16[4,2,8,12,4096]{4,1,3,0,2:T(2,128)(2,1)} %broadcast_select_fusion.1), calls=%async_computation | async-start | bytes 12582912 | tf_op jit(solution)/shard_map/all_to_all | solution.py:34
  122.7 8.0 %copy-start.4 = (s32[8]{0:T(128)S(1)}, s32[8]{0:T(128)}, u32[]{:S(2)}) copy-start(s32[8]{0:T(128)} %param.7) | copy-start | bytes 100
  122.7 148.7 %all-to-all-start.1 = ((bf16[16,4,2,12,4096]{4,2,1,3,0:T(2,128)(2,1)}), bf16[16,4,2,12,4096]{4,2,1,3,0:T(2,128)(2,1)}, u32[]{:S(2)}, u32[]{:S(2)}) async-start(bf16[16,4,2,12,4096]{4,2,1,3,0:T(2,128)(2,1)} %stack.2), calls=%async_computation.1 | async-start | bytes 25165824 | tf_op jit(solution)/shard_map/all_to_all | solution.py:18
  130.5 306.5 %all-gather.2.cloned.1.call-start = ((), (), s32[]{:S(2)}) async-start(), calls=%async_computation.2 | async-start | bytes 13369344 | tf_op jit(solution)/shard_map/all_gather | solution.py:47
  343.8 104.0 %copy-start.2 = (bf16[4,2,12,64,64]{3,4,0,1,2:T(8,128)(2,1)}, bf16[4,2,12,64,64]{3,4,0,1,2:T(8,128)(2,1)S(1)}, u32[]{:S(2)}) copy-start(bf16[4,2,12,64,64]{3,4,0,1,2:T(8,128)(2,1)S(1)} %fusion.11) | copy-start | bytes 2359300
  349.3 241.1 %all-reduce.2.cloned.1.call-start = ((), (), s32[]{:S(2)}) async-start(), calls=%async_computation.3 | async-start | bytes 12582912 | tf_op jit(solution)/shard_map/psum | solution.py:11
  594.5 12.0 %copy-start.1 = (bf16[4,2,47,4096]{3,1,2,0:T(2,128)(2,1)S(1)}, bf16[4,2,47,4096]{3,1,2,0:T(2,128)(2,1)}, u32[]{:S(2)}) copy-start(bf16[4,2,47,4096]{3,1,2,0:T(2,128)(2,1)} %param.5) | copy-start | bytes 9240580
Sparse Core Ops, SparseCore 0:
  349.4 87.5 all-gather.1
  447.9 142.4 all-reduce.1
